TPU v7x, 32 devices: a whole 2x2x4 slice. The times are simulated.
32 devices in a mesh: groups: 2 (over y), row: 16 (over z, x, core).
Axes of the slice: x: 2, y: 2, z: 4, core: 2. Of those that a mesh axis runs over, the one named last changes fastest.
Arguments:
- homolog_activation: float32 [32, 512, 256], P('groups', 'row'), parts along dimension 0, may hold values from -6 to 6
- homolog_entry_valid: int32 [32, 512], P('groups', 'row'), parts along dimension 0, may hold values 0 or 1
- amino_valid_flags: int32 [1024], P(('groups', 'row')), parts along dimension 0, may hold values 0 or 1
- first_factor_weights: float32 [256, 32], replicated, may hold values from -0.375 to 0.375
- second_factor_weights: float32 [256, 32], replicated, may hold values from -0.375 to 0.375
- final_linear_weights: float32 [1024, 128], replicated, may hold values from -0.1875 to 0.1875
- couple_delta_deriv: float32 [1024, 512, 128], P(('groups', 'row')), parts along dimension 0, may hold values from -6 to 6
Outputs:
- alignment_grad: float32 [32, 512, 256], P('groups', 'row'), parts along dimension 0
- left_weight_grad: float32 [512, 32], P('groups'), parts along dimension 0
- right_weight_grad: float32 [512, 32], P('groups'), parts along dimension 0
- out_weight_grad: float32 [2048, 128], P('groups'), parts along dimension 0
There are 2 independent parts, one for each index of `groups`. A program takes and returns all parts, laid end to end along the dimension named above; an argument that names none is the same for every part. Nothing has to cross between parts.
All inputs are finite; a program needn't handle non-finite values. No bound on the sum of `homolog_entry_valid` or of `amino_valid_flags` on one device may be relied on, other than what follows from the above.
Results may differ from a plain program's by a relative error of at most 0.0003.
Values sent between devices are 32-bit elements; how exact they have to be, the bound alone decides.
A program may use at most 128 MiB of HBM per device.

v0:
```python
import jax
import jax.numpy as jnp
from jax import lax
from jax.sharding import PartitionSpec as P

SPLIT_PIECES = lax.Precision.HIGHEST


def local(
    homolog_activation,
    homolog_entry_valid,
    amino_valid_flags,
    first_factor_weights,
    second_factor_weights,
    final_linear_weights,
    couple_delta_deriv,
):
    rows = couple_delta_deriv.shape[0]
    total = couple_delta_deriv.shape[1]
    homolog_number_here = homolog_activation.shape[0]
    width = first_factor_weights.shape[1]
    pair_width = final_linear_weights.shape[1]
    keep_mask = homolog_entry_valid.astype(jnp.float32).T
    present = amino_valid_flags.astype(jnp.float32)
    homolog_slice_here = jnp.transpose(homolog_activation, (1, 0, 2))
    first_factor_embed = (
        jnp.einsum("plg,gz->plz", homolog_slice_here, first_factor_weights, precision=SPLIT_PIECES)
        * keep_mask[:, :, None]
    )
    second_factor_embed = (
        jnp.einsum("plg,gz->plz", homolog_slice_here, second_factor_weights, precision=SPLIT_PIECES)
        * keep_mask[:, :, None]
    )
    right_flat, keep_all, present_all = (
        lax.all_gather(
            second_factor_embed.reshape(rows, homolog_number_here * width),
            "row",
            axis=0,
            tiled=True,
        ),
        lax.all_gather(keep_mask, "row", axis=0, tiled=True),
        lax.all_gather(present, "row", axis=0, tiled=True),
    )
    right_all = right_flat.reshape(total, homolog_number_here, width)
    count = jnp.dot(
        keep_mask, keep_all.T, precision=SPLIT_PIECES, preferred_element_type=jnp.float32
    )
    factor = present[:, None] * present_all[None, :] / jnp.maximum(count, 1.0)
    scaled = couple_delta_deriv * factor[:, :, None]
    w_three = final_linear_weights.reshape(width, width, pair_width)
    block = min(256, total)
    right_pieces = []
    for begin in range(0, total, block):
        piece = scaled[:, begin : begin + block]
        feats = jnp.einsum("rjk,abk->rjab", piece, w_three, precision=SPLIT_PIECES)
        right_pieces.append(
            jnp.einsum("rjab,rsa->jsb", feats, first_factor_embed, precision=SPLIT_PIECES)
        )
    carried = jnp.einsum("rjk,jsc->rsck", scaled, right_all, precision=SPLIT_PIECES)
    output_grad = jnp.einsum("rsa,rsck->ack", first_factor_embed, carried, precision=SPLIT_PIECES)
    first_factor_embed_deriv = jnp.einsum("rsck,ack->rsa", carried, w_three, precision=SPLIT_PIECES)
    right_terms = jnp.concatenate(right_pieces, axis=0)
    summed = lax.psum(right_terms, "row")
    second_factor_embed_deriv = lax.dynamic_slice_in_dim(
        summed, lax.axis_index("row") * rows, rows, 0
    )
    first_factor_embed_deriv = first_factor_embed_deriv * keep_mask[:, :, None]
    second_factor_embed_deriv = second_factor_embed_deriv * keep_mask[:, :, None]
    alignment_grad = jnp.einsum(
        "gyo,fo->ygf", first_factor_embed_deriv, first_factor_weights, precision=SPLIT_PIECES
    ) + jnp.einsum(
        "gyo,fo->ygf", second_factor_embed_deriv, second_factor_weights, precision=SPLIT_PIECES
    )
    first_operand_array = jnp.einsum(
        "dxb,dxo->bo", homolog_slice_here, first_factor_embed_deriv, precision=SPLIT_PIECES
    )
    second_operand_array = jnp.einsum(
        "dxb,dxo->bo", homolog_slice_here, second_factor_embed_deriv, precision=SPLIT_PIECES
    )
    output_grad_total, left_grad_total, right_grad_total = lax.psum(
        (output_grad.reshape(width * width, pair_width), first_operand_array, second_operand_array),
        "row",
    )
    return (alignment_grad, left_grad_total, right_grad_total, output_grad_total)


def solution(mesh):
    in_specs = (
        P("groups", "row", None),
        P("groups", "row"),
        P(("groups", "row")),
        P(),
        P(),
        P(),
        P(("groups", "row"), None, None),
    )
    out_specs = (P("groups", "row", None), P("groups", None), P("groups", None), P("groups", None))
    return jax.shard_map(local, mesh=mesh, in_specs=in_specs, out_specs=out_specs, check_vma=False)
```

profile of v0, /device:TPU:8, one launch (start us, length us, event | category | flops | bytes accessed | tf_op | source)
XLA Modules:
  0.0 453.5 jit_solution(17768828914577271759)
XLA Ops:
  7.2 0.7 convert_bitcast_fusion
  8.0 1.8 convolution_multiply_fusion.1
  9.8 0.8 reshape.24
  10.7 19.3 %all-gather = f32[16,32,16]{1,2,0:T(8,128)S(1)} all-gather(f32[1,32,16]{1,2,0:T(8,128)S(1)} %get-tuple-element.24), channel_id=1, replica_groups=mesh['groups'=2,'row'=16] {'row'}, dimensions={0}, use_global_device_ids=true | all-gather | bytes 34816 | tf_op jit(solution)/shard_map/all_gather | solution.py:41
  30.8 1.2 dynamic-slice
  32.7 0.8 convert_dynamic-update-slice_fusion
  33.4 24.7 %all-reduce = f32[512]{0:T(512)S(1)} all-reduce(f32[512]{0:T(512)S(1)} %convert_dynamic-update-slice_fusion), channel_id=1, replica_groups=mesh['groups'=2,'row'=16] {'row'}, use_global_device_ids=true, to_apply=%add | all-reduce | flops 512 | bytes 4096
  58.1 1.0 fusion.22
  59.0 5.3 %broadcast_multiply_fusion = f32[32,512,128]{2,1,0:T(8,128)S(1)} fusion(f32[32,512,128]{2,1,0:T(8,128)} %param.13, f32[32,512]{1,0:T(8,128)S(1)} %fusion.22), kind=kLoop, calls=%fused_computation.11 | loop fusion | flops 2097152 | bytes 16842752 | tf_op jit(solution)/shard_map/mul | solution.py:49
  64.3 30.6 %fusion.7 = f32[32,256,32,32]{1,2,0,3:T(8,128)} fusion(f32[32,512,128]{2,1,0:T(8,128)S(1)} %broadcast_multiply_fusion, f32[32,32,128,1]{2,1,0,3:T(8,128)S(1)} %bitcast.87), kind=kOutput, calls=%fused_computation.9 | convolution fusion | flops 12884901888 | bytes 38273024 | tf_op jit(solution)/shard_map/rjk,abk->rjab/dot_general | solution.py:55
  95.0 30.8 %fusion.6 = f32[32,256,32,32]{1,2,0,3:T(8,128)} fusion(f32[32,512,128]{2,1,0:T(8,128)S(1)} %broadcast_multiply_fusion, f32[32,32,128,1]{2,1,0,3:T(8,128)S(1)} %bitcast.88), kind=kOutput, calls=%fused_computation.7 | convolution fusion | flops 12884901888 | bytes 38273024 | tf_op jit(solution)/shard_map/rjk,abk->rjab/dot_general | solution.py:55
  125.8 0.8 fusion.18
  126.6 29.3 %convolution_bitcast_fusion.1 = f32[16,256,32]{1,0,2:T(8,128)} fusion(f32[32,16,32,1]{2,1,0,3:T(8,128)S(1)} %fusion.18, f32[32,256,32,32]{1,2,0,3:T(8,128)} %fusion.7), kind=kOutput, calls=%fused_computation.14 | convolution fusion | flops 1610612736 | bytes 34144256 | tf_op jit(solution)/shard_map/rjab,rsa->jsb/dot_general | solution.py:57
  155.9 2.4 copy.68
  158.3 29.5 %convolution_bitcast_fusion = f32[16,256,32]{1,0,2:T(8,128)} fusion(f32[32,16,32,1]{2,1,0,3:T(8,128)S(1)} %fusion.18, f32[32,256,32,32]{1,2,0,3:T(8,128)} %fusion.6), kind=kOutput, calls=%fused_computation.13 | convolution fusion | flops 1610612736 | bytes 34144256 | tf_op jit(solution)/shard_map/rjab,rsa->jsb/dot_general | solution.py:57
  187.9 3.6 copy.70
  191.5 3.8 pad_maximum_fusion
  195.3 1.6 copy.62
  196.9 16.3 %fusion.8 = f32[32,16,32,128]{3,2,0,1:T(8,128)S(1)} fusion(f32[512,16,32,1]{0,2,3,1:T(8,128)S(1)} %bitcast.91, f32[32,512,128]{2,1,0:T(8,128)} %copy-done.2), kind=kOutput, calls=%fused_computation.12 | convolution fusion | flops 12884901888 | bytes 17825792 | tf_op jit(solution)/shard_map/rjk,jsc->rsck/dot_general | solution.py:59
  213.2 3.2 copy-done.1
  216.4 9.4 %fusion.11 = f32[32,32,128]{2,0,1:T(8,128)S(1)} fusion(f32[32,16,32,1]{2,1,0,3:T(8,128)S(1)} %fusion.18, f32[32,16,32,128]{3,2,0,1:T(8,128)S(1)} %fusion.8), kind=kOutput, calls=%fused_computation.15 | convolution fusion | flops 805306368 | bytes 8978432 | tf_op jit(solution)/shard_map/rsa,rsck->ack/dot_general | solution.py:60
  225.9 1.1 copy.74
  227.0 14.3 %fusion.19 = f32[32,16,32]{2,1,0:T(8,128)S(1)} fusion(f32[32,16,32,128]{3,2,0,1:T(8,128)} %copy-done.1, f32[32,32,128]{2,1,0:T(8,128)S(1)} %bitcast.89, f32[32,16]{1,0:T(8,128)S(1)} %copy.61), kind=kOutput, calls=%fused_computation.22 | convolution fusion | flops 805322752 | bytes 8980480 | tf_op jit(solution)/shard_map/rsck,ack->rsa/dot_general | solution.py:61
  241.3 1.4 convolution_bitcast_fusion.3
  243.3 105.7 %all-reduce.8.cloned.1.call-done = (f32[512,16,32]{2,1,0:T(8,128)}, f32[1024,128]{1,0:T(8,128)}) async-done(((f32[512,16,32]{2,1,0:T(8,128)}, f32[1024,128]{1,0:T(8,128)}), (f32[512,16,32]{2,1,0:T(8,128)}, f32[1024,128]{1,0:T(8,128)})) %all-reduce.8.cloned.1.call-update) | async-done | bytes 1572880 | tf_op jit(solution)/shard_map/psum | solution.py:63
  348.9 2.4 convolution_bitcast_fusion.2
  351.4 1.6 fusion.14
  353.0 1.1 copy.75
  354.1 88.0 %all-reduce.6.cloned.1.call-done = (f32[256,32]{0,1:T(8,128)}, f32[256,32]{0,1:T(8,128)}) async-done(((f32[256,32]{0,1:T(8,128)}, f32[256,32]{0,1:T(8,128)}), (f32[256,32]{0,1:T(8,128)}, f32[256,32]{0,1:T(8,128)})) %all-reduce.6.cloned.1.call-update) | async-done | bytes 65552 | tf_op jit(solution)/shard_map/psum | solution.py:80
  442.1 1.4 copy.115
  443.5 1.4 copy.116
  444.9 1.9 copy.117
  (24 shorter events, 1.6 us)
Async XLA Ops:
  7.2 118.6 %copy-start = (f32[256,32]{0,1:T(8,128)S(1)}, f32[256,32]{0,1:T(8,128)}, u32[]{:S(2)}) copy-start(f32[256,32]{0,1:T(8,128)} %param.10) | copy-start | bytes 98308
  7.2 188.1 %all-gather.3.cloned.1.call-start = ((), (), s32[]{:S(2)}) async-start(), calls=%async_computation | async-start | bytes 1114112 | tf_op jit(solution)/shard_map/all_gather | solution.py:35
  10.6 338.3 %all-reduce.8.cloned.1.call-start = ((), (), s32[]{:S(2)}) async-start(), calls=%async_computation.2 | async-start | bytes 9437184 | tf_op jit(solution)/shard_map/psum | solution.py:63
  59.0 5.3 %copy-start.4 = (f32[1024,128]{1,0:T(8,128)S(1)}, f32[1024,128]{1,0:T(8,128)}, u32[]{:S(2)}) copy-start(f32[1024,128]{1,0:T(8,128)} %param.12) | copy-start | bytes 1572868
  64.3 30.7 %copy-start.2 = (f32[32,512,128]{2,1,0:T(8,128)}, f32[32,512,128]{2,1,0:T(8,128)S(1)}, u32[]{:S(2)}) copy-start(f32[32,512,128]{2,1,0:T(8,128)S(1)} %broadcast_multiply_fusion) | copy-start | bytes 25165828
  95.0 30.8 %copy-start.3 = (f32[16,32,256]{2,1,0:T(8,128)S(1)}, f32[16,32,256]{2,1,0:T(8,128)}, u32[]{:S(2)}) copy-start(f32[16,32,256]{2,1,0:T(8,128)} %param.7) | copy-start | bytes 1572868
  213.2 3.2 copy-start.1
  227.0 124.4 %copy-start.5 = (f32[256,32]{0,1:T(8,128)S(1)}, f32[256,32]{0,1:T(8,128)}, u32[]{:S(2)}) copy-start(f32[256,32]{0,1:T(8,128)} %param.11) | copy-start | bytes 98308
  227.0 215.1 %all-reduce.6.cloned.1.call-start = ((), (), s32[]{:S(2)}) async-start(), calls=%async_computation.1 | async-start | bytes 131072 | tf_op jit(solution)/shard_map/psum | solution.py:80
Sparse Core Ops, SparseCore 0:
  10.8 38.1 all-gather.2
  227.1 121.7 all-reduce.7
  353.1 89.0 all-reduce.5
where the time goes:
time: 461 us; the launch traced here: 453 us
  waiting for transfers between devices  194 us (42%)
  matrix products  170 us (37%)
  blocking collectives  43.9 us (10%)
  local copies, waits for them, and re-layouts  19.9 us (4%)
  between operations  14.7 us (3%)
  other arithmetic  11.2 us (2%)
    psum x1, waiting for transfers between devices, local(): summed = lax.psum(right_terms, 'row')  106 us
    psum x1, waiting for transfers between devices, local(): lax.psum((output_grad.reshape(width * width, pair_width), first_operand_a...  88 us
    dot_general x2, matrix products, local(): feats = jnp.einsum('rjk,abk->rjab', piece, w_three, precision=SPLIT_PIECES)  61.4 us
    dot_general x2, matrix products, local(): jnp.einsum('rjab,rsa->jsb', feats, first_factor_embed, precision=SPLIT_PI...  58.9 us
    unnamed x1, blocking collectives  24.7 us
    all_gather x1, blocking collectives, local(): lax.all_gather(keep_mask, 'row', axis=0, tiled=True)  19.3 us
    dot_general x1, matrix products, local(): jnp.einsum('rjk,jsc->rsck', scaled, right_all, precision=SPLIT_PIECES)  16.3 us
    dot_general x1, matrix products, local(): jnp.einsum('rsck,ack->rsa', carried, w_three, precision=SPLIT_PIECES)  14.3 us
  transfers between devices with their start and end apart: 3, of which 2 were waited for; matrix products, arithmetic and copies ran while one was open for 35% of the time, Pallas kernels for 0%

commit v1 on v0

--- a/solution.py
+++ b/solution.py
@@ -60,7 +60,9 @@
     output_grad = jnp.einsum("rsa,rsck->ack", first_factor_embed, carried, precision=SPLIT_PIECES)
     first_factor_embed_deriv = jnp.einsum("rsck,ack->rsa", carried, w_three, precision=SPLIT_PIECES)
     right_terms = jnp.concatenate(right_pieces, axis=0)
-    summed = lax.psum(right_terms, "row")
+    summed = right_terms
+    for hop in (1, 2, 4, 8):
+        summed = summed + lax.ppermute(summed, "row", [(dev, dev ^ hop) for dev in range(16)])
     second_factor_embed_deriv = lax.dynamic_slice_in_dim(
         summed, lax.axis_index("row") * rows, rows, 0
     )

time: 461 us -> 527 us (1.14)
  waiting for transfers between devices: 194 us -> 229 us
  matrix products: 170 us -> 196 us
  starting transfers between devices: 0.12 us -> 9.6 us
    psum x1 -> x0, waiting for transfers between devices: 106 us -> none  [local(): summed = lax.psum(right_terms, 'row')]
    psum x1 -> x2, waiting for transfers between devices: 88 us -> 179 us  [local(): lax.psum((output_grad.reshape(width * width, pair_width), first_operand_a...]
    ppermute x0 -> x4, waiting for transfers between devices: none -> 38.4 us  [local(): lax.ppermute(summed, 'row', [(dev, dev ^ hop) for dev in range(16)])]
    dot_general x2, matrix products: 58.9 us -> 88.7 us  [local(): jnp.einsum('rjab,rsa->jsb', feats, first_factor_embed, precision=SPLIT_PI...]
    all_gather x1, waiting for transfers between devices: 0.01 us -> 11.1 us  [local(): lax.all_gather(second_factor_embed.reshape(rows, homolog_number_here * wi...]
    ppermute x0 -> x4, starting transfers between devices: none -> 9.48 us  [local(): lax.ppermute(summed, 'row', [(dev, dev ^ hop) for dev in range(16)])]
    dot_general x2 -> x1, local copies, waits for them, and re-layouts: 6.01 us -> 0.16 us  [local(): jnp.einsum('rsck,ack->rsa', carried, w_three, precision=SPLIT_PIECES)]
  transfers between devices with their start and end apart: 3 -> 7, of which waited for: 2 -> 6; matrix products, arithmetic and copies ran while one was open for 35% -> 10% of each run, Pallas kernels for 0% -> 0%
where the time goes in v1:
time: 527 us; the launch traced here: 521 us
  waiting for transfers between devices  229 us (43%)
  matrix products  196 us (37%)
  blocking collectives  43.7 us (8%)
  local copies, waits for them, and re-layouts  15.8 us (3%)
  between operations  14.8 us (3%)
  other arithmetic  11.8 us (2%)
  starting transfers between devices  9.6 us (2%)
    psum x2, waiting for transfers between devices, local(): lax.psum((output_grad.reshape(width * width, pair_width), first_operand_a...  179 us
    dot_general x2, matrix products, local(): jnp.einsum('rjab,rsa->jsb', feats, first_factor_embed, precision=SPLIT_PI...  88.7 us
    dot_general x2, matrix products, local(): feats = jnp.einsum('rjk,abk->rjab', piece, w_three, precision=SPLIT_PIECES)  60.3 us
    ppermute x4, waiting for transfers between devices, local(): lax.ppermute(summed, 'row', [(dev, dev ^ hop) for dev in range(16)])  38.4 us
    unnamed x1, blocking collectives  24.6 us
    all_gather x1, blocking collectives, local(): lax.all_gather(keep_mask, 'row', axis=0, tiled=True)  19.1 us
    dot_general x1, matrix products, local(): jnp.einsum('rjk,jsc->rsck', scaled, right_all, precision=SPLIT_PIECES)  16.6 us
    dot_general x1, matrix products, local(): jnp.einsum('rsa,rsck->ack', first_factor_embed, carried, precision=SPLIT_...  12.7 us
  transfers between devices with their start and end apart: 7, of which 6 were waited for; matrix products, arithmetic and copies ran while one was open for 10% of the time, Pallas kernels for 0%

profile of v1, /device:TPU:8, one launch (start us, length us, event | category | flops | bytes accessed | tf_op | source)
XLA Modules:
  0.0 520.5 jit_solution(4388591096407419124)
XLA Ops:
  8.0 19.1 %all-gather = f32[16,32,16]{1,2,0:T(8,128)S(1)} all-gather(f32[1,32,16]{1,2,0:T(8,128)S(1)} %get-tuple-element.32), channel_id=1, replica_groups=mesh['groups'=2,'row'=16] {'row'}, dimensions={0}, use_global_device_ids=true | all-gather | bytes 34816 | tf_op jit(solution)/shard_map/all_gather | solution.py:41
  27.9 1.2 dynamic-slice
  30.6 24.6 %all-reduce = f32[512]{0:T(512)S(1)} all-reduce(f32[512]{0:T(512)S(1)} %convert_dynamic-update-slice_fusion), channel_id=1, replica_groups=mesh['groups'=2,'row'=16] {'row'}, use_global_device_ids=true, to_apply=%add | all-reduce | flops 512 | bytes 4096
  56.2 5.3 %broadcast_multiply_fusion = f32[32,512,128]{2,1,0:T(8,128)S(1)} fusion(f32[32,512,128]{2,1,0:T(8,128)} %param.13, f32[32,512]{1,0:T(8,128)S(1)} %fusion.28), kind=kLoop, calls=%fused_computation.14 | loop fusion | flops 2097152 | bytes 16842752 | tf_op jit(solution)/shard_map/mul | solution.py:49
  61.5 30.1 %fusion.11 = f32[32,256,32,32]{1,3,2,0:T(8,128)} fusion(f32[32,32,128,1]{2,1,0,3:T(8,128)S(1)} %bitcast.100, f32[32,512,128]{2,1,0:T(8,128)S(1)} %broadcast_multiply_fusion), kind=kOutput, calls=%fused_computation.13 | convolution fusion | flops 12884901888 | bytes 38273024 | tf_op jit(solution)/shard_map/rjk,abk->rjab/dot_general | solution.py:55
  91.6 30.2 %fusion.10 = f32[32,256,32,32]{1,3,2,0:T(8,128)} fusion(f32[32,32,128,1]{2,1,0,3:T(8,128)S(1)} %bitcast.101, f32[32,512,128]{2,1,0:T(8,128)S(1)} %broadcast_multiply_fusion), kind=kOutput, calls=%fused_computation.11 | convolution fusion | flops 12884901888 | bytes 38273024 | tf_op jit(solution)/shard_map/rjk,abk->rjab/dot_general | solution.py:55
  121.8 1.3 convolution_multiply_fusion
  123.1 50.2 %fusion.15 = f32[16,256,32]{1,0,2:T(8,128)S(1)} fusion(f32[32,256,32,32]{1,3,2,0:T(8,128)} %fusion.11, f32[32,16,32]{0,2,1:T(8,128)S(1)} %convolution_multiply_fusion), kind=kOutput, calls=%fused_computation.16 | convolution fusion | flops 1610612736 | bytes 34144256 | tf_op jit(solution)/shard_map/rjab,rsa->jsb/dot_general | solution.py:57
  173.3 38.5 %fusion.18 = f32[16,256,32]{1,0,2:T(8,128)S(1)} fusion(f32[32,256,32,32]{1,3,2,0:T(8,128)S(1)} %copy-done.1, f32[32,16,32]{0,2,1:T(8,128)S(1)} %convolution_multiply_fusion), kind=kOutput, calls=%fused_computation.17 | convolution fusion | flops 1610612736 | bytes 34144256 | tf_op jit(solution)/shard_map/rjab,rsa->jsb/dot_general | solution.py:57
  212.7 2.6 collective-permute-done
  215.6 1.3 convolution_multiply_fusion.1
  217.7 23.9 %collective-permute-done.1 = f32[512,16,32]{0,2,1:T(8,128)} collective-permute-done((f32[512,16,32]{0,2,1:T(8,128)S(1)}, f32[512,16,32]{0,2,1:T(8,128)}, u32[]{:S(2)}, u32[]{:S(2)}) %collective-permute-start.1) | collective-permute-done | bytes 1048608 | tf_op jit(solution)/shard_map/ppermute | solution.py:65
  241.6 1.4 add.28
  243.0 8.5 %collective-permute-start.2 = (f32[512,16,32]{0,2,1:T(8,128)S(1)}, f32[512,16,32]{0,2,1:T(8,128)}, u32[]{:S(2)}, u32[]{:S(2)}) collective-permute-start(f32[512,16,32]{0,2,1:T(8,128)S(1)} %add.28), channel_id=1, source_target_pairs={{0,4},{1,5},{2,6},{3,7},{4,0},{5,1},{6,2},{7,3},{8,12},{9,13},{10,... | collective-permute-start | bytes 3145736 | tf_op jit(solution)/shard_map/ppermute | solution.py:65
  251.6 11.1 %all-gather.3.cloned.1.call-done = f32[512,512]{1,0:T(8,128)} async-done(((f32[32,512]{1,0:T(8,128)}), f32[512,512]{1,0:T(8,128)}) %all-gather.3.cloned.1.call-update) | async-done | bytes 1048592 | tf_op jit(solution)/shard_map/all_gather | solution.py:35
  262.7 2.5 copy.118
  265.2 11.9 %collective-permute-done.2 = f32[512,16,32]{0,2,1:T(8,128)} collective-permute-done((f32[512,16,32]{0,2,1:T(8,128)S(1)}, f32[512,16,32]{0,2,1:T(8,128)}, u32[]{:S(2)}, u32[]{:S(2)}) %collective-permute-start.2) | collective-permute-done | bytes 1048608 | tf_op jit(solution)/shard_map/ppermute | solution.py:65
  277.1 1.4 add.29
  279.3 16.6 %fusion.12 = f32[32,16,32,128]{3,2,0,1:T(8,128)S(1)} fusion(f32[512,16,32,1]{0,2,3,1:T(8,128)} %bitcast.105, f32[32,512,128]{2,1,0:T(8,128)} %copy-done.2), kind=kOutput, calls=%fused_computation.15 | convolution fusion | flops 12884901888 | bytes 17825792 | tf_op jit(solution)/shard_map/rjk,jsc->rsck/dot_general | solution.py:59
  296.0 3.2 copy-done.3
  299.2 10.9 %fusion.25 = f32[32,16,32]{2,1,0:T(8,128)S(1)} fusion(f32[32,16,32,128]{3,2,0,1:T(8,128)S(1)} %fusion.12, f32[32,32,128]{2,1,0:T(8,128)S(1)} %bitcast.102), kind=kOutput, calls=%fused_computation.21 | convolution fusion | flops 805306368 | bytes 8978432 | tf_op jit(solution)/shard_map/rsck,ack->rsa/dot_general | solution.py:61
  310.2 12.7 %fusion.21 = f32[32,32,128]{2,0,1:T(8,128)S(1)} fusion(f32[32,16,32,128]{3,2,0,1:T(8,128)} %copy-done.3, f32[32,16,32]{0,2,1:T(8,128)S(1)} %convolution_multiply_fusion), kind=kOutput, calls=%fused_computation.18 | convolution fusion | flops 805306368 | bytes 8978432 | tf_op jit(solution)/shard_map/rsa,rsck->ack/dot_general | solution.py:60
  323.0 1.1 copy.134
  324.2 1.2 fusion.35
  325.3 1.1 convolution_bitcast_fusion
  326.4 1.1 convolution_bitcast_fusion.1
  329.0 1.1 copy.135
  330.1 86.8 %all-reduce.5.cloned.1.call-done = f32[1024,128]{1,0:T(8,128)} async-done(((f32[1024,128]{1,0:T(8,128)}), f32[1024,128]{1,0:T(8,128)}) %all-reduce.5.cloned.1.call-update) | async-done | bytes 524304 | tf_op jit(solution)/shard_map/psum | solution.py:82
  416.9 92.3 %all-reduce.7.cloned.1.call-done = (f32[256,32]{0,1:T(8,128)}, f32[256,32]{0,1:T(8,128)}) async-done(((f32[256,32]{0,1:T(8,128)}, f32[256,32]{0,1:T(8,128)}), (f32[256,32]{0,1:T(8,128)}, f32[256,32]{0,1:T(8,128)})) %all-reduce.7.cloned.1.call-update) | async-done | bytes 65552 | tf_op jit(solution)/shard_map/psum | solution.py:82
  509.2 1.4 copy.181
  510.5 1.4 copy.182
  511.9 1.9 copy.183
  (39 shorter events, 7.7 us)
Async XLA Ops:
  7.2 114.6 %copy-start = (f32[16,32,256]{2,1,0:T(8,128)S(1)}, f32[16,32,256]{2,1,0:T(8,128)}, u32[]{:S(2)}) copy-start(f32[16,32,256]{2,1,0:T(8,128)} %param.7) | copy-start | bytes 1572868
  7.2 255.5 %all-gather.3.cloned.1.call-start = ((), (), s32[]{:S(2)}) async-start(), calls=%async_computation | async-start | bytes 1114112 | tf_op jit(solution)/shard_map/all_gather | solution.py:35
  56.2 5.3 %copy-start.4 = (f32[1024,128]{1,0:T(8,128)S(1)}, f32[1024,128]{1,0:T(8,128)}, u32[]{:S(2)}) copy-start(f32[1024,128]{1,0:T(8,128)} %param.12) | copy-start | bytes 1572868
  61.4 30.1 %copy-start.2 = (f32[32,512,128]{2,1,0:T(8,128)}, f32[32,512,128]{2,1,0:T(8,128)S(1)}, u32[]{:S(2)}) copy-start(f32[32,512,128]{2,1,0:T(8,128)S(1)} %broadcast_multiply_fusion) | copy-start | bytes 25165828
  91.6 30.2 %copy-start.5 = (f32[256,32]{0,1:T(8,128)S(1)}, f32[256,32]{0,1:T(8,128)}, u32[]{:S(2)}) copy-start(f32[256,32]{0,1:T(8,128)} %param.10) | copy-start | bytes 98308
  123.1 50.2 %copy-start.1 = (f32[32,256,32,32]{1,3,2,0:T(8,128)S(1)}, f32[32,256,32,32]{1,3,2,0:T(8,128)}, u32[]{:S(2)}) copy-start(f32[32,256,32,32]{1,3,2,0:T(8,128)} %fusion.10) | copy-start | bytes 100663296
  173.3 42.3 %copy-start.6 = (f32[256,32]{0,1:T(8,128)S(1)}, f32[256,32]{0,1:T(8,128)}, u32[]{:S(2)}) copy-start(f32[256,32]{0,1:T(8,128)} %param.11) | copy-start | bytes 98308
  212.6 2.7 collective-permute-start
  215.5 26.1 %collective-permute-start.1 = (f32[512,16,32]{0,2,1:T(8,128)S(1)}, f32[512,16,32]{0,2,1:T(8,128)}, u32[]{:S(2)}, u32[]{:S(2)}) collective-permute-start(f32[512,16,32]{0,2,1:T(8,128)S(1)} %fusion.47), channel_id=1, source_target_pairs={{0,2},{1,3},{2,0},{3,1},{4,6},{5,7},{6,4},{7,5},{8,10},{9,11},{10,... | collective-permute-start | bytes 3145736 | tf_op jit(solution)/shard_map/ppermute | solution.py:65
  217.7 199.2 %all-reduce.5.cloned.1.call-start = ((), (), s32[]{:S(2)}) async-start(), calls=%async_computation.1 | async-start | bytes 1048576 | tf_op jit(solution)/shard_map/psum | solution.py:82
  243.0 34.0 %collective-permute-start.2 = (f32[512,16,32]{0,2,1:T(8,128)S(1)}, f32[512,16,32]{0,2,1:T(8,128)}, u32[]{:S(2)}, u32[]{:S(2)}) collective-permute-start(f32[512,16,32]{0,2,1:T(8,128)S(1)} %add.28), channel_id=1, source_target_pairs={{0,4},{1,5},{2,6},{3,7},{4,0},{5,1},{6,2},{7,3},{8,12},{9,13},{10,... | collective-permute-start | bytes 3145736 | tf_op jit(solution)/shard_map/ppermute | solution.py:65
  278.5 45.6 %collective-permute-start.3 = (f32[512,16,32]{0,2,1:T(8,128)S(1)}, f32[512,16,32]{0,2,1:T(8,128)}, u32[]{:S(2)}, u32[]{:S(2)}) collective-permute-start(f32[512,16,32]{0,2,1:T(8,128)S(1)} %add.29), channel_id=1, source_target_pairs={{0,8},{1,9},{2,10},{3,11},{4,12},{5,13},{6,14},{7,15},{8,0},{9,1},... | collective-permute-start | bytes 3145736 | tf_op jit(solution)/shard_map/ppermute | solution.py:65
  295.9 3.2 copy-start.3
  324.1 185.1 %all-reduce.7.cloned.1.call-start = ((), (), s32[]{:S(2)}) async-start(), calls=%async_computation.2 | async-start | bytes 131072 | tf_op jit(solution)/shard_map/psum | solution.py:82
Sparse Core Ops, SparseCore 0:
  217.8 44.8 all-gather.2
  324.2 92.6 all-reduce.4
  421.0 88.0 all-reduce.6
